TPU v7x, 32 devices: a whole 2x2x4 slice. The times are simulated.
32 devices in a mesh: row: 8 (over z, y), col: 4 (over x, core).
Axes of the slice: x: 2, y: 2, z: 4, core: 2. Of those that a mesh axis runs over, the one named last changes fastest.
Arguments:
- tensor_ri: bfloat16 [8, 8, 4, 128, 1152], P('row', None, 'col'), may hold values from -6 to 6
- block_mask: int32 [8, 4, 9], P('row', 'col'), may hold values 0 or 1
- green_virt: bfloat16 [8, 4, 128, 3200], P('row', 'col'), may hold values from -0.1875 to 0.1875
- green_occ: bfloat16 [8, 4, 128, 128], P('row', 'col'), may hold values from -0.5 to 0.5
Outputs:
- response: float32 [8, 8], replicated
All inputs are finite; a program needn't handle non-finite values. No bound on the sum of `block_mask` on one device may be relied on, other than what follows from the above.
Results may differ from a plain program's by a relative error of at most 0.0044.
Values may be sent and summed in bfloat16 or wider, within the bound.
A program may use at most 192 MiB of HBM per device.

v0:
```python
import math
import jax
import jax.numpy as jnp
from jax import lax
from jax.sharding import PartitionSpec as P


def extended(cells, sides, width):
    for axis, dim in sides:
        count = lax.axis_size(axis)
        ends = count - 1
        head = lax.slice_in_dim(cells, 0, width, axis=dim)
        tail = lax.slice_in_dim(cells, cells.shape[dim] - width, cells.shape[dim], axis=dim)
        cells = jnp.concatenate(
            [
                lax.ppermute(tail, axis, [(i, (i + 1) % count) for i in range(ends)]),
                cells,
                lax.ppermute(head, axis, [((i + 1) % count, i) for i in range(ends)]),
            ],
            axis=dim,
        )
    return cells


def window_of(band, src_row, src_col, block_width):
    grid_band = band.reshape(block_width, 5, 5, block_width)
    picked = grid_band[:, 2 - src_row : 5 - src_row, 2 - src_col : 5 - src_col, :]
    return picked.reshape(block_width, 9 * block_width)


def per_device(tensor_ri, block_mask, green_virt, green_occ):
    row_count = lax.axis_size("row")
    col_count = lax.axis_size("col")
    block_width = green_occ.shape[-1]
    pair_width = tensor_ri.shape[-1]
    occ_block = green_occ[0, 0]
    regrouped = lax.all_to_all(tensor_ri, "row", split_axis=1, concat_axis=0, tiled=True)
    occ_applied = jnp.einsum(
        "ji,pabiw->pabjw", occ_block, regrouped, preferred_element_type=jnp.float32
    ).astype(jnp.bfloat16)
    rows_all = regrouped.shape[0]
    regrouped = regrouped.reshape(rows_all, block_width, pair_width)
    occ_applied = occ_applied.reshape(rows_all, block_width, pair_width)
    grid_row = lax.axis_index("row")
    grid_col = lax.axis_index("col")
    slots = jnp.arange(9, dtype=jnp.int32)
    near_row = grid_row + slots // 3 - 1
    near_col = grid_col + slots % 3 - 1
    usable = (
        (block_mask[0, 0] == 1)
        & (near_row >= 0)
        & (near_row < row_count)
        & (near_col >= 0)
        & (near_col < col_count)
    )
    kept_slots = jnp.repeat(usable.astype(jnp.bfloat16), block_width)
    regrouped = regrouped * kept_slots
    occ_applied = occ_applied * kept_slots
    windows = []
    rim_blocks = extended(green_virt, (("row", 0), ("col", 1)), 1)
    for source in range(9):
        src_row, src_col = (source // 3, source % 3)
        windows.append(window_of(rim_blocks[src_row, src_col], src_row, src_col, block_width))
    flat_rows = regrouped.reshape(rows_all * block_width, pair_width)
    half_sum = jnp.zeros((rows_all * block_width, pair_width), jnp.float32)
    for source in range(9):
        tile = flat_rows[:, source * block_width : (source + 1) * block_width]
        half_sum = half_sum + jnp.dot(tile, windows[source], preferred_element_type=jnp.float32)
    half_done = half_sum.astype(jnp.bfloat16).reshape(rows_all, block_width * pair_width)
    occ_flat = occ_applied.reshape(rows_all, block_width * pair_width)
    partial_value = lax.dot_general(
        half_done, occ_flat, (((1,), (1,)), ((), ())), preferred_element_type=jnp.float32
    )
    total_basis = block_width * row_count * col_count
    response = lax.psum(partial_value, ("row", "col"))
    return response * (1.0 / math.sqrt(total_basis * 9 * block_width))


def solution(mesh):
    return jax.shard_map(
        per_device,
        mesh=mesh,
        in_specs=(
            P("row", None, "col", None, None),
            P("row", "col", None),
            P("row", "col", None, None),
            P("row", "col", None, None),
        ),
        out_specs=P(),
        check_vma=False,
    )
```

profile of v0, /device:TPU:10, one launch (start us, length us, event | category | flops | bytes accessed | tf_op | source)
XLA Modules:
  0.0 181.1 jit_solution(1390845295951888833)
XLA Ops:
  0.0 0.0 copy-start
  0.0 1.7 copy.15
  1.7 0.0 copy-start.3
  1.7 3.4 %collective-permute-start.1 = (bf16[1,1,128,3200]{2,3,1,0:T(8,128)(2,1)S(1)}, bf16[1,1,128,3200]{2,3,1,0:T(8,128)(2,1)S(1)}, u32[]{:S(2)}, u32[]{:S(2)}) collective-permute-start(bf16[1,1,128,3200]{2,3,1,0:T(8,128)(2,1)S(1)} %copy.15), channel_id=1, source_target_pairs={{4,0},{8,4},{12,8},{16,12},{20,16},{24,20},{28,24},{5,1},{9,5},{13... | collective-permute-start | bytes 2457608 | tf_op jit(solution)/shard_map/ppermute | solution.py:18
  5.2 2.5 %collective-permute-start = (bf16[1,1,128,3200]{2,3,1,0:T(8,128)(2,1)S(1)}, bf16[1,1,128,3200]{2,3,1,0:T(8,128)(2,1)S(1)}, u32[]{:S(2)}, u32[]{:S(2)}) collective-permute-start(bf16[1,1,128,3200]{2,3,1,0:T(8,128)(2,1)S(1)} %copy.15), channel_id=1, source_target_pairs={{0,4},{4,8},{8,12},{12,16},{16,20},{20,24},{24,28},{1,5},{5,9},{9,... | collective-permute-start | bytes 2457608 | tf_op jit(solution)/shard_map/ppermute | solution.py:16
  7.7 33.6 %collective-permute-done.1 = bf16[1,1,128,3200]{2,3,1,0:T(8,128)(2,1)S(1)} collective-permute-done((bf16[1,1,128,3200]{2,3,1,0:T(8,128)(2,1)S(1)}, bf16[1,1,128,3200]{2,3,1,0:T(8,128)(2,1)S(1)}, u32[]{:S(2)}, u32[]{:S(2)}) %collective-permute-start.1) | collective-permute-done | bytes 819232 | tf_op jit(solution)/shard_map/ppermute | solution.py:18
  41.3 0.0 copy-start.4
  41.3 0.0 collective-permute-done
  41.3 0.9 copy-done.4
  42.2 0.0 copy-start.5
  42.2 1.7 pad_maximum_fusion
  43.9 0.0 copy-done.5
  43.9 1.9 %collective-permute-start.3 = (bf16[3,1,128,3200]{2,3,1,0:T(8,128)(2,1)}, bf16[3,1,128,3200]{2,3,1,0:T(8,128)(2,1)}, u32[]{:S(2)}, u32[]{:S(2)}) collective-permute-start(bf16[3,1,128,3200]{2,3,1,0:T(8,128)(2,1)} %pad_maximum_fusion), channel_id=1, source_target_pairs={{1,0},{2,1},{3,2},{5,4},{6,5},{7,6},{9,8},{10,9},{11,10},{13,12},{... | collective-permute-start | bytes 7372808 | tf_op jit(solution)/shard_map/ppermute | solution.py:18
  45.9 0.0 copy-done.3
  45.9 2.6 %copy.13 = bf16[1,8,1,128,1152]{3,4,2,0,1:T(8,128)(2,1)} copy(bf16[1,8,1,128,1152]{4,3,2,1,0:T(8,128)(2,1)S(1)} %copy-done.3) | data formatting | bytes 4718592 | tf_op args[0]
  48.4 0.0 copy-start.12
  48.4 5.5 %all-to-all-start = ((bf16[1,8,1,128,1152]{3,4,2,0,1:T(8,128)(2,1)}), bf16[1,8,1,128,1152]{3,4,2,0,1:T(8,128)(2,1)S(1)}, u32[]{:S(2)}, u32[]{:S(2)}) async-start(bf16[1,8,1,128,1152]{3,4,2,0,1:T(8,128)(2,1)} %copy.13), calls=%async_computation | async-start | bytes 4718592 | tf_op jit(solution)/shard_map/all_to_all | solution.py:37
  54.0 3.2 %collective-permute-start.2 = (bf16[3,1,128,3200]{2,3,1,0:T(8,128)(2,1)}, bf16[3,1,128,3200]{2,3,1,0:T(8,128)(2,1)}, u32[]{:S(2)}, u32[]{:S(2)}) collective-permute-start(bf16[3,1,128,3200]{2,3,1,0:T(8,128)(2,1)} %pad_maximum_fusion), channel_id=1, source_target_pairs={{0,1},{1,2},{2,3},{4,5},{5,6},{6,7},{8,9},{9,10},{10,11},{12,13},{... | collective-permute-start | bytes 7372808 | tf_op jit(solution)/shard_map/ppermute | solution.py:16
  57.2 0.0 copy-done.12
  57.2 0.1 broadcast_bitcast_fusion
  57.3 1.0 slice.116
  58.3 1.7 slice.100
  60.0 13.6 %collective-permute-done.3 = bf16[3,1,128,3200]{2,3,1,0:T(8,128)(2,1)} collective-permute-done((bf16[3,1,128,3200]{2,3,1,0:T(8,128)(2,1)}, bf16[3,1,128,3200]{2,3,1,0:T(8,128)(2,1)}, u32[]{:S(2)}, u32[]{:S(2)}) %collective-permute-start.3) | collective-permute-done | bytes 2457632 | tf_op jit(solution)/shard_map/ppermute | solution.py:18
  73.6 1.8 fusion.27
  75.4 0.7 slice.119
  76.1 0.7 slice.103
  76.9 8.6 %collective-permute-done.2 = bf16[3,1,128,3200]{2,3,1,0:T(8,128)(2,1)} collective-permute-done((bf16[3,1,128,3200]{2,3,1,0:T(8,128)(2,1)}, bf16[3,1,128,3200]{2,3,1,0:T(8,128)(2,1)}, u32[]{:S(2)}, u32[]{:S(2)}) %collective-permute-start.2) | collective-permute-done | bytes 2457632 | tf_op jit(solution)/shard_map/ppermute | solution.py:16
  85.5 1.8 fusion.26
  87.3 0.7 slice.114
  88.0 0.8 slice.106
  88.8 0.7 slice.98
  89.5 17.2 %all-to-all-done = bf16[1,8,1,128,1152]{3,4,2,0,1:T(8,128)(2,1)S(1)} async-done(((bf16[1,8,1,128,1152]{3,4,2,0,1:T(8,128)(2,1)}), bf16[1,8,1,128,1152]{3,4,2,0,1:T(8,128)(2,1)S(1)}, u32[]{:S(2)}, u32[]{:S(2)}) %all-to-all-start) | async-done | bytes 2359328 | tf_op jit(solution)/shard_map/all_to_all | solution.py:37
  106.7 2.6 %copy.14 = bf16[1,8,1,128,1152]{4,3,1,2,0:T(8,128)(2,1)} copy(bf16[1,8,1,128,1152]{3,4,2,0,1:T(8,128)(2,1)S(1)} %all-to-all-done) | data formatting | bytes 4718592 | tf_op jit(solution)/shard_map/all_to_all | solution.py:37
  109.3 3.3 %bitcast_multiply_fusion = bf16[1024,1152]{1,0:T(8,128)(2,1)} fusion(bf16[1,8,1,128,1152]{4,3,1,2,0:T(8,128)(2,1)} %copy.14, bf16[1152]{0:T(1024)(128)(2,1)S(1)} %broadcast_bitcast_fusion), kind=kLoop, calls=%fused_computation.15 | loop fusion | flops 1179648 | bytes 4720896 | tf_op jit(solution)/shard_map/mul | solution.py:57
  112.6 0.0 copy-done
  112.6 2.2 %fusion.4 = bf16[8,1,1,128,1152]{3,4,0,2,1:T(8,128)(2,1)} fusion(bf16[1,8,1,128,1152]{3,4,2,0,1:T(8,128)(2,1)S(1)} %all-to-all-done, bf16[1152]{0:T(1024)(128)(2,1)S(1)} %broadcast_bitcast_fusion, bf16[1,1,128,128]{3,2,1,0:T(8,128)(2,1)S(1)} %copy-done), kind=kOutput, calls=%fused_computation.12 | convolution fusion | flops 304349184 | bytes 4753664 | tf_op jit(solution)/shard_map/ji,pabiw->pabjw/dot_general | solution.py:38
  114.8 4.3 %copy.19 = bf16[8,1,1,128,1152]{4,3,0,2,1:T(8,128)(2,1)} copy(bf16[8,1,1,128,1152]{3,4,0,2,1:T(8,128)(2,1)} %fusion.4) | data formatting | bytes 4718592 | tf_op jit(solution)/shard_map/mul | solution.py:58
  119.1 0.0 copy-start.2
  119.1 0.0 copy-start.9
  119.1 3.1 %copy.20 = bf16[1,8,128,1152]{3,1,2,0:T(8,128)(2,1)S(1)} copy(bf16[1,8,128,1152]{3,2,1,0:T(8,128)(2,1)} %bitcast.64) | data formatting | bytes 4718592
  122.3 0.0 copy-done.2
  122.3 0.0 copy-done.9
  122.3 0.0 copy-start.6
  122.3 0.8 fusion.6
  123.1 0.2 copy-done.6
  123.3 0.0 copy-start.11
  123.3 0.8 fusion.14
  124.0 0.2 copy-done.11
  124.2 0.8 convolution_add_fusion.6
  125.0 0.2 copy-done.8
  125.2 0.8 convolution_add_fusion.5
  126.0 0.1 copy-done.10
  126.1 0.8 convolution_add_fusion.4
  126.9 0.8 convolution_add_fusion.3
  127.7 0.0 copy-start.7
  127.7 0.8 convolution_add_fusion.2
  128.5 0.2 copy-done.7
  128.7 0.8 convolution_add_fusion.1
  129.5 2.2 %fusion.1 = bf16[1024,1152]{1,0:T(8,128)(2,1)} fusion(f32[1024,1152]{1,0:T(8,128)S(1)} %fusion.6, f32[1024,1152]{1,0:T(8,128)S(1)} %convolution_add_fusion.1, bf16[128,1152]{0,1:T(8,128)(2,1)S(1)} %bitcast.74, bf16[1024,1152]{1,0:T(8,128)(2,1)S(1)} %copy-done.2), kind=kOutput, calls=%fused_computation.8 | convolution fusion | flops 305528832 | bytes 12353536 | tf_op jit(solution)/shard_map/dot_general | solution.py:68
  131.7 4.1 %reshape.69 = bf16[8,147456]{1,0:T(8,128)(2,1)} reshape(bf16[1024,1152]{1,0:T(8,128)(2,1)} %fusion.1) | data formatting | bytes 4718592 | tf_op jit(solution)/shard_map/reshape | solution.py:69
  135.9 3.3 %fusion.28 = f32[8,8]{1,0:T(8,128)S(1)} fusion(bf16[8,147456]{1,0:T(8,128)(2,1)} %reshape.69, bf16[8,147456]{1,0:T(8,128)(2,1)S(1)} %bitcast.63), kind=kOutput, calls=%fused_computation.46 | convolution fusion | flops 18874368 | bytes 4718848 | tf_op jit(solution)/shard_map/dot_general | solution.py:71
  139.1 41.3 %psum.7 = f32[8,8]{1,0:T(8,128)S(1)} all-reduce(f32[8,8]{1,0:T(8,128)S(1)} %fusion.28), channel_id=1, replica_groups=mesh['row'=8,'col'=4] {'row','col'}, use_global_device_ids=true, to_apply=%region_0.1 | all-reduce | flops 64 | bytes 512 | tf_op jit(solution)/shard_map/psum | solution.py:75
  180.5 0.6 broadcast_multiply_fusion
  181.1 0.0 copy-done.1
  (6 shorter events, 0.1 us)
Async XLA Ops:
  0.0 112.6 %copy-start = (bf16[1,1,128,128]{3,2,1,0:T(8,128)(2,1)S(1)}, bf16[1,1,128,128]{3,2,1,0:T(8,128)(2,1)}, u32[]{:S(2)}) copy-start(bf16[1,1,128,128]{3,2,1,0:T(8,128)(2,1)} %param.7) | copy-start | bytes 98308
  1.7 44.1 %copy-start.3 = (bf16[1,8,1,128,1152]{4,3,2,1,0:T(8,128)(2,1)S(1)}, bf16[1,8,1,128,1152]{4,3,2,1,0:T(8,128)(2,1)}, u32[]{:S(2)}) copy-start(bf16[1,8,1,128,1152]{4,3,2,1,0:T(8,128)(2,1)} %param.4) | copy-start | bytes 7077892
  1.7 39.6 %collective-permute-start.1 = (bf16[1,1,128,3200]{2,3,1,0:T(8,128)(2,1)S(1)}, bf16[1,1,128,3200]{2,3,1,0:T(8,128)(2,1)S(1)}, u32[]{:S(2)}, u32[]{:S(2)}) collective-permute-start(bf16[1,1,128,3200]{2,3,1,0:T(8,128)(2,1)S(1)} %copy.15), channel_id=1, source_target_pairs={{4,0},{8,4},{12,8},{16,12},{20,16},{24,20},{28,24},{5,1},{9,5},{13... | collective-permute-start | bytes 2457608 | tf_op jit(solution)/shard_map/ppermute | solution.py:18
  5.2 36.1 %collective-permute-start = (bf16[1,1,128,3200]{2,3,1,0:T(8,128)(2,1)S(1)}, bf16[1,1,128,3200]{2,3,1,0:T(8,128)(2,1)S(1)}, u32[]{:S(2)}, u32[]{:S(2)}) collective-permute-start(bf16[1,1,128,3200]{2,3,1,0:T(8,128)(2,1)S(1)} %copy.15), channel_id=1, source_target_pairs={{0,4},{4,8},{8,12},{12,16},{16,20},{20,24},{24,28},{1,5},{5,9},{9,... | collective-permute-start | bytes 2457608 | tf_op jit(solution)/shard_map/ppermute | solution.py:16
  41.3 0.9 copy-start.4
  42.2 1.7 copy-start.5
  43.9 29.6 %collective-permute-start.3 = (bf16[3,1,128,3200]{2,3,1,0:T(8,128)(2,1)}, bf16[3,1,128,3200]{2,3,1,0:T(8,128)(2,1)}, u32[]{:S(2)}, u32[]{:S(2)}) collective-permute-start(bf16[3,1,128,3200]{2,3,1,0:T(8,128)(2,1)} %pad_maximum_fusion), channel_id=1, source_target_pairs={{1,0},{2,1},{3,2},{5,4},{6,5},{7,6},{9,8},{10,9},{11,10},{13,12},{... | collective-permute-start | bytes 7372808 | tf_op jit(solution)/shard_map/ppermute | solution.py:18
  48.4 8.8 %copy-start.12 = (s32[1,1,9]{2,1,0:T(1,128)S(1)}, s32[1,1,9]{2,1,0:T(1,128)}, u32[]{:S(2)}) copy-start(s32[1,1,9]{2,1,0:T(1,128)} %param.5) | copy-start | bytes 112
  48.4 58.3 %all-to-all-start = ((bf16[1,8,1,128,1152]{3,4,2,0,1:T(8,128)(2,1)}), bf16[1,8,1,128,1152]{3,4,2,0,1:T(8,128)(2,1)S(1)}, u32[]{:S(2)}, u32[]{:S(2)}) async-start(bf16[1,8,1,128,1152]{3,4,2,0,1:T(8,128)(2,1)} %copy.13), calls=%async_computation | async-start | bytes 4718592 | tf_op jit(solution)/shard_map/all_to_all | solution.py:37
  54.0 31.5 %collective-permute-start.2 = (bf16[3,1,128,3200]{2,3,1,0:T(8,128)(2,1)}, bf16[3,1,128,3200]{2,3,1,0:T(8,128)(2,1)}, u32[]{:S(2)}, u32[]{:S(2)}) collective-permute-start(bf16[3,1,128,3200]{2,3,1,0:T(8,128)(2,1)} %pad_maximum_fusion), channel_id=1, source_target_pairs={{0,1},{1,2},{2,3},{4,5},{5,6},{6,7},{8,9},{9,10},{10,11},{12,13},{... | collective-permute-start | bytes 7372808 | tf_op jit(solution)/shard_map/ppermute | solution.py:16
  119.1 3.1 %copy-start.2 = (bf16[1024,1152]{1,0:T(8,128)(2,1)S(1)}, bf16[1024,1152]{1,0:T(8,128)(2,1)}, u32[]{:S(2)}) copy-start(bf16[1024,1152]{1,0:T(8,128)(2,1)} %bitcast_multiply_fusion) | copy-start | bytes 7077892
  119.1 3.1 %copy-start.9 = (bf16[128,3,3,128]{0,3,2,1:T(8,128)(2,1)S(1)}, bf16[128,3,3,128]{0,3,2,1:T(8,128)(2,1)}, u32[]{:S(2)}) copy-start(bf16[128,3,3,128]{0,3,2,1:T(8,128)(2,1)} %slice.119) | copy-start | bytes 884740
  122.3 1.0 copy-start.6
  123.3 1.0 copy-start.11
  124.2 1.0 copy-start.8
  125.2 1.0 copy-start.10
  127.7 1.0 copy-start.7
  131.7 49.4 %copy-start.1 = (bf16[1,1,128,128]{3,2,1,0:T(8,128)(2,1)S(1)}, bf16[1,1,128,128]{3,2,1,0:T(8,128)(2,1)}, u32[]{:S(2)}) copy-start(bf16[1,1,128,128]{3,2,1,0:T(8,128)(2,1)} %param.7) | copy-start | bytes 98308
where the time goes:
time: 182 us; the launch traced here: 181 us
  waiting for transfers between devices  72.9 us (40%)
  blocking collectives  41.3 us (23%)
  local copies, waits for them, and re-layouts  30.4 us (17%)
  starting transfers between devices  16.6 us (9%)
  matrix products  14 us (8%)
  other arithmetic  5.65 us (3%)
    ppermute x2, waiting for transfers between devices, extended(): lax.ppermute(head, axis, [((i + 1) % count, i) for i in range(ends)])  47.1 us
    psum x1, blocking collectives, per_device(): response = lax.psum(partial_value, ('row', 'col'))  41.3 us
    all_to_all x1, waiting for transfers between devices, per_device(): lax.all_to_all(tensor_ri, 'row', split_axis=1, concat_axis=0, tiled=True)  17.2 us
    unnamed x29, local copies, waits for them, and re-layouts  9.19 us
    ppermute x2, waiting for transfers between devices, extended(): lax.ppermute(tail, axis, [(i, (i + 1) % count) for i in range(ends)])  8.6 us
    dot_general x9, matrix products, per_device(): jnp.dot(tile, windows[source], preferred_element_type=jnp.float32)  8.5 us
    slice x9, local copies, waits for them, and re-layouts, window_of(): picked = grid_band[:, 2 - src_row:5 - src_row, 2 - src_col:5 - src_col, :]  6.45 us
    ppermute x2, starting transfers between devices, extended(): lax.ppermute(tail, axis, [(i, (i + 1) % count) for i in range(ends)])  5.74 us
  transfers between devices with their start and end apart: 5, of which 4 were waited for; matrix products, arithmetic and copies ran while one was open for 7% of the time, Pallas kernels for 0%

commit v1 on v0

--- a/solution.py
+++ b/solution.py
@@ -72,7 +72,8 @@
         half_done, occ_flat, (((1,), (1,)), ((), ())), preferred_element_type=jnp.float32
     )
     total_basis = block_width * row_count * col_count
-    response = lax.psum(partial_value, ("row", "col"))
+    parts = lax.all_gather(partial_value, ("row", "col"), axis=0, tiled=False)
+    response = parts.sum(axis=0)
     return response * (1.0 / math.sqrt(total_basis * 9 * block_width))
 
 

time: 182 us -> 184 us (1.011)
  the two profiles are of different devices: /device:TPU:10 before, /device:TPU:0 now
where the time goes in v1:
time: 184 us; the launch traced here: 183 us
  waiting for transfers between devices  75 us (41%)
  blocking collectives  40.4 us (22%)
  local copies, waits for them, and re-layouts  29.5 us (16%)
  starting transfers between devices  18.5 us (10%)
  matrix products  14 us (8%)
  other arithmetic  5.69 us (3%)
    all_to_all x1, waiting for transfers between devices, per_device(): lax.all_to_all(tensor_ri, 'row', split_axis=1, concat_axis=0, tiled=True)  41 us
    all_gather x1, blocking collectives, per_device(): parts = lax.all_gather(partial_value, ('row', 'col'), axis=0, tiled=False)  40.4 us
    ppermute x2, waiting for transfers between devices, extended(): lax.ppermute(tail, axis, [(i, (i + 1) % count) for i in range(ends)])  17.7 us
    ppermute x2, waiting for transfers between devices, extended(): lax.ppermute(head, axis, [((i + 1) % count, i) for i in range(ends)])  16.3 us
    ppermute x2, starting transfers between devices, extended(): lax.ppermute(tail, axis, [(i, (i + 1) % count) for i in range(ends)])  9.79 us
    dot_general x9, matrix products, per_device(): jnp.dot(tile, windows[source], preferred_element_type=jnp.float32)  8.48 us
    unnamed x29, local copies, waits for them, and re-layouts  8.29 us
    slice x9, local copies, waits for them, and re-layouts, window_of(): picked = grid_band[:, 2 - src_row:5 - src_row, 2 - src_col:5 - src_col, :]  6.45 us
  transfers between devices with their start and end apart: 5, of which 3 were waited for; matrix products, arithmetic and copies ran while one was open for 7% of the time, Pallas kernels for 0%

profile of v1, /device:TPU:0, one launch (start us, length us, event | category | flops | bytes accessed | tf_op | source)
XLA Modules:
  0.0 183.2 jit_solution(15184007008995038226)
XLA Ops:
  0.0 0.0 copy-start
  0.0 1.7 copy.15
  1.7 0.0 copy-start.3
  1.7 1.4 collective-permute-start.1
  3.2 5.6 %collective-permute-start = (bf16[1,1,128,3200]{2,3,1,0:T(8,128)(2,1)S(1)}, bf16[1,1,128,3200]{2,3,1,0:T(8,128)(2,1)S(1)}, u32[]{:S(2)}, u32[]{:S(2)}) collective-permute-start(bf16[1,1,128,3200]{2,3,1,0:T(8,128)(2,1)S(1)} %copy.15), channel_id=1, source_target_pairs={{0,4},{4,8},{8,12},{12,16},{16,20},{20,24},{24,28},{1,5},{5,9},{9,... | collective-permute-start | bytes 2457608 | tf_op jit(solution)/shard_map/ppermute | solution.py:16
  8.7 16.3 %collective-permute-done.1 = bf16[1,1,128,3200]{2,3,1,0:T(8,128)(2,1)S(1)} collective-permute-done((bf16[1,1,128,3200]{2,3,1,0:T(8,128)(2,1)S(1)}, bf16[1,1,128,3200]{2,3,1,0:T(8,128)(2,1)S(1)}, u32[]{:S(2)}, u32[]{:S(2)}) %collective-permute-start.1) | collective-permute-done | bytes 819232 | tf_op jit(solution)/shard_map/ppermute | solution.py:18
  25.0 0.0 copy-start.4
  25.0 17.7 %collective-permute-done = bf16[1,1,128,3200]{2,3,1,0:T(8,128)(2,1)S(1)} collective-permute-done((bf16[1,1,128,3200]{2,3,1,0:T(8,128)(2,1)S(1)}, bf16[1,1,128,3200]{2,3,1,0:T(8,128)(2,1)S(1)}, u32[]{:S(2)}, u32[]{:S(2)}) %collective-permute-start) | collective-permute-done | bytes 819232 | tf_op jit(solution)/shard_map/ppermute | solution.py:16
  42.7 0.0 copy-done.4
  42.7 0.0 copy-start.5
  42.7 1.7 pad_maximum_fusion
  44.4 0.0 copy-done.5
  44.4 1.3 collective-permute-start.3
  45.7 0.0 copy-done.3
  45.7 2.6 %copy.13 = bf16[1,8,1,128,1152]{3,4,2,0,1:T(8,128)(2,1)} copy(bf16[1,8,1,128,1152]{4,3,2,1,0:T(8,128)(2,1)S(1)} %copy-done.3) | data formatting | bytes 4718592 | tf_op args[0]
  48.3 0.0 copy-start.12
  48.3 6.0 %all-to-all-start = ((bf16[1,8,1,128,1152]{3,4,2,0,1:T(8,128)(2,1)}), bf16[1,8,1,128,1152]{3,4,2,0,1:T(8,128)(2,1)S(1)}, u32[]{:S(2)}, u32[]{:S(2)}) async-start(bf16[1,8,1,128,1152]{3,4,2,0,1:T(8,128)(2,1)} %copy.13), calls=%async_computation | async-start | bytes 4718592 | tf_op jit(solution)/shard_map/all_to_all | solution.py:37
  54.3 4.2 %collective-permute-start.2 = (bf16[3,1,128,3200]{2,3,1,0:T(8,128)(2,1)}, bf16[3,1,128,3200]{2,3,1,0:T(8,128)(2,1)}, u32[]{:S(2)}, u32[]{:S(2)}) collective-permute-start(bf16[3,1,128,3200]{2,3,1,0:T(8,128)(2,1)} %pad_maximum_fusion), channel_id=1, source_target_pairs={{0,1},{1,2},{2,3},{4,5},{5,6},{6,7},{8,9},{9,10},{10,11},{12,13},{... | collective-permute-start | bytes 7372808 | tf_op jit(solution)/shard_map/ppermute | solution.py:16
  58.5 0.0 copy-done.12
  58.5 0.1 broadcast_bitcast_fusion
  58.6 1.0 slice.116
  59.6 1.7 slice.100
  61.3 0.0 collective-permute-done.3
  61.3 1.8 fusion.27
  63.1 0.7 slice.119
  63.9 0.7 slice.103
  64.6 0.0 collective-permute-done.2
  64.6 1.8 fusion.26
  66.4 0.7 slice.114
  67.2 0.8 slice.106
  67.9 0.7 slice.98
  68.7 41.0 %all-to-all-done = bf16[1,8,1,128,1152]{3,4,2,0,1:T(8,128)(2,1)S(1)} async-done(((bf16[1,8,1,128,1152]{3,4,2,0,1:T(8,128)(2,1)}), bf16[1,8,1,128,1152]{3,4,2,0,1:T(8,128)(2,1)S(1)}, u32[]{:S(2)}, u32[]{:S(2)}) %all-to-all-start) | async-done | bytes 2359328 | tf_op jit(solution)/shard_map/all_to_all | solution.py:37
  109.7 2.6 %copy.14 = bf16[1,8,1,128,1152]{4,3,1,2,0:T(8,128)(2,1)} copy(bf16[1,8,1,128,1152]{3,4,2,0,1:T(8,128)(2,1)S(1)} %all-to-all-done) | data formatting | bytes 4718592 | tf_op jit(solution)/shard_map/all_to_all | solution.py:37
  112.3 3.3 %bitcast_multiply_fusion = bf16[1024,1152]{1,0:T(8,128)(2,1)} fusion(bf16[1,8,1,128,1152]{4,3,1,2,0:T(8,128)(2,1)} %copy.14, bf16[1152]{0:T(1024)(128)(2,1)S(1)} %broadcast_bitcast_fusion), kind=kLoop, calls=%fused_computation.15 | loop fusion | flops 1179648 | bytes 4720896 | tf_op jit(solution)/shard_map/mul | solution.py:57
  115.6 0.0 copy-done
  115.6 2.2 %fusion.4 = bf16[8,1,1,128,1152]{3,4,0,2,1:T(8,128)(2,1)} fusion(bf16[1,8,1,128,1152]{3,4,2,0,1:T(8,128)(2,1)S(1)} %all-to-all-done, bf16[1152]{0:T(1024)(128)(2,1)S(1)} %broadcast_bitcast_fusion, bf16[1,1,128,128]{3,2,1,0:T(8,128)(2,1)S(1)} %copy-done), kind=kOutput, calls=%fused_computation.12 | convolution fusion | flops 304349184 | bytes 4753664 | tf_op jit(solution)/shard_map/ji,pabiw->pabjw/dot_general | solution.py:38
  117.8 4.3 %copy.19 = bf16[8,1,1,128,1152]{4,3,0,2,1:T(8,128)(2,1)} copy(bf16[8,1,1,128,1152]{3,4,0,2,1:T(8,128)(2,1)} %fusion.4) | data formatting | bytes 4718592 | tf_op jit(solution)/shard_map/mul | solution.py:58
  122.1 0.0 copy-start.2
  122.1 3.1 %copy.20 = bf16[1,8,128,1152]{3,1,2,0:T(8,128)(2,1)S(1)} copy(bf16[1,8,128,1152]{3,2,1,0:T(8,128)(2,1)} %bitcast.66) | data formatting | bytes 4718592
  125.2 0.0 copy-done.2
  125.2 0.0 copy-done.9
  125.3 0.0 copy-start.6
  125.3 0.8 fusion.6
  126.0 0.2 copy-done.6
  126.2 0.8 fusion.14
  127.0 0.2 copy-done.11
  127.2 0.0 copy-start.8
  127.2 0.8 convolution_add_fusion.6
  128.0 0.2 copy-done.8
  128.1 0.0 copy-start.10
  128.1 0.8 convolution_add_fusion.5
  128.9 0.2 copy-done.10
  129.1 0.8 convolution_add_fusion.4
  129.9 0.8 convolution_add_fusion.3
  130.7 0.0 copy-start.7
  130.7 0.8 convolution_add_fusion.2
  131.5 0.2 copy-done.7
  131.7 0.8 convolution_add_fusion.1
  132.5 2.2 %fusion.1 = bf16[1024,1152]{1,0:T(8,128)(2,1)} fusion(f32[1024,1152]{1,0:T(8,128)S(1)} %fusion.6, f32[1024,1152]{1,0:T(8,128)S(1)} %convolution_add_fusion.1, bf16[128,1152]{0,1:T(8,128)(2,1)S(1)} %bitcast.76, bf16[1024,1152]{1,0:T(8,128)(2,1)S(1)} %copy-done.2), kind=kOutput, calls=%fused_computation.8 | convolution fusion | flops 305528832 | bytes 12353536 | tf_op jit(solution)/shard_map/dot_general | solution.py:68
  134.7 4.1 %reshape.69 = bf16[8,147456]{1,0:T(8,128)(2,1)} reshape(bf16[1024,1152]{1,0:T(8,128)(2,1)} %fusion.1) | data formatting | bytes 4718592 | tf_op jit(solution)/shard_map/reshape | solution.py:69
  138.8 3.3 %fusion.28 = f32[8,8]{1,0:T(8,128)S(1)} fusion(bf16[8,147456]{1,0:T(8,128)(2,1)} %reshape.69, bf16[8,147456]{1,0:T(8,128)(2,1)S(1)} %bitcast.65), kind=kOutput, calls=%fused_computation.47 | convolution fusion | flops 18874368 | bytes 4718848 | tf_op jit(solution)/shard_map/dot_general | solution.py:71
  142.1 40.4 %all-gather = f32[256,8]{1,0:T(8,128)S(1)} all-gather(f32[8,8]{1,0:T(8,128)S(1)} %fusion.28), channel_id=2, replica_groups=mesh['row'=8,'col'=4] {'row','col'}, dimensions={0}, use_global_device_ids=true | all-gather | bytes 8448 | tf_op jit(solution)/shard_map/all_gather | solution.py:75
  182.6 0.6 broadcast_multiply_fusion
  183.2 0.0 copy-done.1
  (7 shorter events, 0.1 us)
Async XLA Ops:
  0.0 115.6 %copy-start = (bf16[1,1,128,128]{3,2,1,0:T(8,128)(2,1)S(1)}, bf16[1,1,128,128]{3,2,1,0:T(8,128)(2,1)}, u32[]{:S(2)}) copy-start(bf16[1,1,128,128]{3,2,1,0:T(8,128)(2,1)} %param.7) | copy-start | bytes 98308
  1.7 44.0 %copy-start.3 = (bf16[1,8,1,128,1152]{4,3,2,1,0:T(8,128)(2,1)S(1)}, bf16[1,8,1,128,1152]{4,3,2,1,0:T(8,128)(2,1)}, u32[]{:S(2)}) copy-start(bf16[1,8,1,128,1152]{4,3,2,1,0:T(8,128)(2,1)} %param.4) | copy-start | bytes 7077892
  1.7 23.2 %collective-permute-start.1 = (bf16[1,1,128,3200]{2,3,1,0:T(8,128)(2,1)S(1)}, bf16[1,1,128,3200]{2,3,1,0:T(8,128)(2,1)S(1)}, u32[]{:S(2)}, u32[]{:S(2)}) collective-permute-start(bf16[1,1,128,3200]{2,3,1,0:T(8,128)(2,1)S(1)} %copy.15), channel_id=1, source_target_pairs={{4,0},{8,4},{12,8},{16,12},{20,16},{24,20},{28,24},{5,1},{9,5},{13... | collective-permute-start | bytes 2457608 | tf_op jit(solution)/shard_map/ppermute | solution.py:18
  3.2 39.5 %collective-permute-start = (bf16[1,1,128,3200]{2,3,1,0:T(8,128)(2,1)S(1)}, bf16[1,1,128,3200]{2,3,1,0:T(8,128)(2,1)S(1)}, u32[]{:S(2)}, u32[]{:S(2)}) collective-permute-start(bf16[1,1,128,3200]{2,3,1,0:T(8,128)(2,1)S(1)} %copy.15), channel_id=1, source_target_pairs={{0,4},{4,8},{8,12},{12,16},{16,20},{20,24},{24,28},{1,5},{5,9},{9,... | collective-permute-start | bytes 2457608 | tf_op jit(solution)/shard_map/ppermute | solution.py:16
  25.0 17.7 %copy-start.4 = (bf16[1,1,128,3200]{2,3,1,0:T(8,128)(2,1)}, bf16[1,1,128,3200]{2,3,1,0:T(8,128)(2,1)S(1)}, u32[]{:S(2)}) copy-start(bf16[1,1,128,3200]{2,3,1,0:T(8,128)(2,1)S(1)} %collective-permute-done.1) | copy-start | bytes 2457604
  42.7 1.7 copy-start.5
  44.4 16.9 %collective-permute-start.3 = (bf16[3,1,128,3200]{2,3,1,0:T(8,128)(2,1)}, bf16[3,1,128,3200]{2,3,1,0:T(8,128)(2,1)}, u32[]{:S(2)}, u32[]{:S(2)}) collective-permute-start(bf16[3,1,128,3200]{2,3,1,0:T(8,128)(2,1)} %pad_maximum_fusion), channel_id=1, source_target_pairs={{1,0},{2,1},{3,2},{5,4},{6,5},{7,6},{9,8},{10,9},{11,10},{13,12},{... | collective-permute-start | bytes 7372808 | tf_op jit(solution)/shard_map/ppermute | solution.py:18
  48.3 10.2 %copy-start.12 = (s32[1,1,9]{2,1,0:T(1,128)S(1)}, s32[1,1,9]{2,1,0:T(1,128)}, u32[]{:S(2)}) copy-start(s32[1,1,9]{2,1,0:T(1,128)} %param.5) | copy-start | bytes 112
  48.3 61.4 %all-to-all-start = ((bf16[1,8,1,128,1152]{3,4,2,0,1:T(8,128)(2,1)}), bf16[1,8,1,128,1152]{3,4,2,0,1:T(8,128)(2,1)S(1)}, u32[]{:S(2)}, u32[]{:S(2)}) async-start(bf16[1,8,1,128,1152]{3,4,2,0,1:T(8,128)(2,1)} %copy.13), calls=%async_computation | async-start | bytes 4718592 | tf_op jit(solution)/shard_map/all_to_all | solution.py:37
  54.3 10.4 %collective-permute-start.2 = (bf16[3,1,128,3200]{2,3,1,0:T(8,128)(2,1)}, bf16[3,1,128,3200]{2,3,1,0:T(8,128)(2,1)}, u32[]{:S(2)}, u32[]{:S(2)}) collective-permute-start(bf16[3,1,128,3200]{2,3,1,0:T(8,128)(2,1)} %pad_maximum_fusion), channel_id=1, source_target_pairs={{0,1},{1,2},{2,3},{4,5},{5,6},{6,7},{8,9},{9,10},{10,11},{12,13},{... | collective-permute-start | bytes 7372808 | tf_op jit(solution)/shard_map/ppermute | solution.py:16
  122.1 3.1 %copy-start.2 = (bf16[1024,1152]{1,0:T(8,128)(2,1)S(1)}, bf16[1024,1152]{1,0:T(8,128)(2,1)}, u32[]{:S(2)}) copy-start(bf16[1024,1152]{1,0:T(8,128)(2,1)} %bitcast_multiply_fusion) | copy-start | bytes 7077892
  122.1 3.1 %copy-start.9 = (bf16[128,3,3,128]{0,3,2,1:T(8,128)(2,1)S(1)}, bf16[128,3,3,128]{0,3,2,1:T(8,128)(2,1)}, u32[]{:S(2)}) copy-start(bf16[128,3,3,128]{0,3,2,1:T(8,128)(2,1)} %slice.119) | copy-start | bytes 884740
  125.3 1.0 copy-start.6
  126.2 1.0 copy-start.11
  127.2 1.0 copy-start.8
  128.1 1.0 copy-start.10
  130.7 1.0 copy-start.7
  138.8 44.4 %copy-start.1 = (bf16[1,1,128,128]{3,2,1,0:T(8,128)(2,1)S(1)}, bf16[1,1,128,128]{3,2,1,0:T(8,128)(2,1)}, u32[]{:S(2)}) copy-start(bf16[1,1,128,128]{3,2,1,0:T(8,128)(2,1)} %param.7) | copy-start | bytes 98308
